TPU v7x, 32 devices: a whole 2x2x4 slice. The times are simulated.
32 devices in a mesh: parts: 2 (over y), tm: 4 (over z), space: 4 (over x, core).
Axes of the slice: x: 2, y: 2, z: 4, core: 2. Of those that a mesh axis runs over, the one named last changes fastest.
Arguments:
- rhs: float32 [8, 16, 16, 1024], P(('parts', 'tm'), None, 'space'), parts along dimension 0, may hold values from -24 to 24
- diffusivity: float32 [32, 16, 1024], P('parts', 'space'), parts along dimension 0, may hold values from 0.5 to 2
- velocity: float32 [6], P('parts'), parts along dimension 0, may hold values from -1 to 1
Outputs:
- solution: float32 [8, 16, 16, 1024], P(('parts', 'tm'), None, 'space'), parts along dimension 0
There are 2 independent parts, one for each index of `parts`. A program takes and returns all parts, laid end to end along the dimension named above; each array names one. Nothing has to cross between parts.
All inputs are finite; a program needn't handle non-finite values.
Results may differ from a plain program's by a relative error of at most 0.0002.
Values sent between devices are 32-bit elements; how exact they have to be, the bound alone decides.
No kernel may reach another device: no remote copies, remote signals or barrier semaphores. Data moves between devices by JAX's collectives and lax.ppermute only.
A program may use at most 64 MiB of HBM per device.

v0:
```python
import math
import jax
import jax.numpy as jnp
from jax import lax
from jax.sharding import PartitionSpec as P

circ_alpha = 0.1
relax_weights = (
    1.0 / (1.0 - 0.5 * math.cos(math.pi / 8.0)),
    1.0 / (1.0 - 0.5 * math.cos(3.0 * math.pi / 8.0)),
    1.0 / (1.0 - 0.5 * math.cos(5.0 * math.pi / 8.0)),
    1.0 / (1.0 - 0.5 * math.cos(7.0 * math.pi / 8.0)),
)


def padded(shard, sides, width):
    for axis, dim in sides:
        size, length = (lax.axis_size(axis), shard.shape[dim])
        up = [(i, (i + 1) % size) for i in range(size - 1)]
        down = [(j, i) for i, j in up]
        last = lax.slice_in_dim(shard, length - width, length, axis=dim)
        initial = lax.slice_in_dim(shard, 0, width, axis=dim)
        before = lax.ppermute(last, axis, up)
        after = lax.ppermute(initial, axis, down)
        shard = jnp.concatenate([before, shard, after], axis=dim)
    return shard


def stencil(extended, diffusivity, diag_re, diag_im, velocity):
    center = extended[:, :, :, 1:-1, :]
    upper_y = extended[:, :, :, 2:, :]
    lower_y = extended[:, :, :, :-2, :]
    zero_z = jnp.zeros_like(center[:, :, :1])
    upper_z = jnp.concatenate([center[:, :, 1:], zero_z], axis=2)
    lower_z = jnp.concatenate([zero_z, center[:, :, :-1]], axis=2)
    zero_x = jnp.zeros_like(center[:, :, :, :, :1])
    upper_x = jnp.concatenate([center[:, :, :, :, 1:], zero_x], axis=4)
    lower_x = jnp.concatenate([zero_x, center[:, :, :, :, :-1]], axis=4)
    coefficient = diffusivity[None, None]
    half_velocity = 0.5 * velocity
    beside = (coefficient - half_velocity[0]) * upper_z + (coefficient + half_velocity[0]) * lower_z
    beside = (
        beside
        + (coefficient - half_velocity[1]) * upper_y
        + (coefficient + half_velocity[1]) * lower_y
    )
    beside = (
        beside
        + (coefficient - half_velocity[2]) * upper_x
        + (coefficient + half_velocity[2]) * lower_x
    )
    denominator = diag_re + 6.0 * diffusivity
    center_re = center[:, 0]
    center_im = center[:, 1]
    total_re = denominator * center_re - diag_im * center_im
    total_im = denominator * center_im + diag_im * center_re
    return jnp.stack([total_re, total_im], axis=1) - beside


def divide(residual, diffusivity, diag_re, diag_im):
    denominator = diag_re + 6.0 * diffusivity
    modulus = denominator * denominator + diag_im * diag_im
    residual_re = residual[:, 0]
    residual_im = residual[:, 1]
    quotient_re = (residual_re * denominator + residual_im * diag_im) / modulus
    quotient_im = (residual_im * denominator - residual_re * diag_im) / modulus
    return jnp.stack([quotient_re, quotient_im], axis=1)


def highest(left, right):
    return jnp.dot(left, right, precision=lax.Precision.HIGHEST, preferred_element_type=jnp.float32)


def twiddle(row_index, column_index, length):
    product = row_index[:, None] * column_index[None, :] % length
    phase_table = product.astype(jnp.float32) * (2.0 * math.pi / length)
    return (jnp.cos(phase_table), jnp.sin(phase_table))


def local(rhs, diffusivity, velocity):
    local_steps, depth, rows_y, rows_x = rhs.shape
    length = local_steps * lax.axis_size("tm")
    first_step = lax.axis_index("tm") * local_steps
    own_index = first_step + jnp.arange(local_steps, dtype=jnp.int32)
    log_alpha = math.log(circ_alpha) / length
    cell_count = depth * rows_y * rows_x
    scaled = (
        rhs.reshape(local_steps, cell_count)
        * jnp.exp(own_index.astype(jnp.float32) * log_alpha)[:, None]
    )
    regrouped = lax.all_to_all(scaled, "tm", split_axis=1, concat_axis=0, tiled=True)
    full_index = jnp.arange(length, dtype=jnp.int32)
    cosine_table, sine_table = twiddle(full_index, full_index, length)
    spectrum_re = highest(cosine_table, regrouped)
    spectrum_im = -highest(sine_table, regrouped)
    source_re, source_im = (
        lax.all_to_all(spectrum_re, "tm", split_axis=0, concat_axis=1, tiled=True),
        lax.all_to_all(spectrum_im, "tm", split_axis=0, concat_axis=1, tiled=True),
    )
    source = jnp.stack([source_re, source_im], axis=1).reshape(
        local_steps, 2, depth, rows_y, rows_x
    )
    phase_angle = own_index.astype(jnp.float32) * (2.0 * math.pi / length)
    shift_factor = circ_alpha ** (1.0 / length)
    diag_re = (1.0 - shift_factor * jnp.cos(phase_angle))[:, None, None, None]
    diag_im = (shift_factor * jnp.sin(phase_angle))[:, None, None, None]
    field = relax_weights[0] * divide(source, diffusivity, diag_re, diag_im)
    for weight in relax_weights[1:]:
        extended = padded(field, (("space", 3),), 1)
        applied = stencil(extended, diffusivity, diag_re, diag_im, velocity)
        field = field + weight * divide(source - applied, diffusivity, diag_re, diag_im)
    field_re = field[:, 0].reshape(local_steps, cell_count)
    field_im = field[:, 1].reshape(local_steps, cell_count)
    mixed_re, mixed_im = (
        lax.all_to_all(field_re, "tm", split_axis=1, concat_axis=0, tiled=True),
        lax.all_to_all(field_im, "tm", split_axis=1, concat_axis=0, tiled=True),
    )
    values = (highest(cosine_table, mixed_re) - highest(sine_table, mixed_im)) / length
    restored = lax.all_to_all(values, "tm", split_axis=0, concat_axis=1, tiled=True)
    result = restored * jnp.exp(-own_index.astype(jnp.float32) * log_alpha)[:, None]
    return result.reshape(local_steps, depth, rows_y, rows_x)


def solution(mesh):
    return jax.shard_map(
        local,
        mesh=mesh,
        in_specs=(P(("parts", "tm"), None, "space", None), P("parts", "space", None), P("parts")),
        out_specs=P(("parts", "tm"), None, "space", None),
        check_vma=False,
    )
```

profile of v0, /device:TPU:0, one launch (start us, length us, event | category | flops | bytes accessed | tf_op | source)
XLA Modules:
  0.0 120.9 jit_solution(13436231676874819901)
XLA Ops:
  1.4 15.0 %all_to_all.84 = f32[1,4,16384]{2,0,1:T(1,128)S(1)} all-to-all(f32[1,4,16384]{2,0,1:T(1,128)S(1)} %mul.497), channel_id=1, replica_groups=mesh['parts'=2,'tm'=4,'space'=4] {'tm'}, dimensions={1} | all-to-all | bytes 524288 | tf_op jit(solution)/shard_map/all_to_all | solution.py:91
  18.1 3.4 %all-to-all-start.1 = ((f32[4,1,16384]{2,1,0:T(1,128)}), f32[4,1,16384]{2,1,0:T(1,128)S(1)}, u32[]{:S(2)}, u32[]{:S(2)}) async-start(f32[4,1,16384]{2,1,0:T(1,128)} %copy.4), calls=%async_computation.1 | async-start | bytes 524288 | tf_op jit(solution)/shard_map/all_to_all | solution.py:97
  23.2 6.3 %all-to-all-done.1 = f32[4,1,16384]{2,1,0:T(1,128)S(1)} async-done(((f32[4,1,16384]{2,1,0:T(1,128)}), f32[4,1,16384]{2,1,0:T(1,128)S(1)}, u32[]{:S(2)}, u32[]{:S(2)}) %all-to-all-start.1) | async-done | bytes 262176 | tf_op jit(solution)/shard_map/all_to_all | solution.py:97
  29.5 3.4 %all-to-all-start.2 = ((f32[4,1,16384]{2,1,0:T(1,128)}), f32[4,1,16384]{2,1,0:T(1,128)S(1)}, u32[]{:S(2)}, u32[]{:S(2)}) async-start(f32[4,1,16384]{2,1,0:T(1,128)} %copy.5), calls=%async_computation.2 | async-start | bytes 524288 | tf_op jit(solution)/shard_map/all_to_all | solution.py:98
  36.2 3.4 %all-to-all-done.2 = f32[4,1,16384]{2,1,0:T(1,128)S(1)} async-done(((f32[4,1,16384]{2,1,0:T(1,128)}), f32[4,1,16384]{2,1,0:T(1,128)S(1)}, u32[]{:S(2)}, u32[]{:S(2)}) %all-to-all-start.2) | async-done | bytes 262176 | tf_op jit(solution)/shard_map/all_to_all | solution.py:98
  41.4 2.3 %fusion.38 = (f32[1,1,16,4,1024]{4,3,2,1,0:T(4,128)S(1)}, f32[1,1,16,4,1024]{4,3,2,1,0:T(4,128)S(1)}, f32[16,4,1024]{2,1,0:T(4,128)S(1)}, f32[16,4,1024]{2,1,0:T...) fusion(f32[16,4,1024]{2,1,0:T(4,128)S(1)} %squeeze.67, ...), kind=kLoop, calls=%fused_computation.79 | loop fusion | flops 1179648 | bytes 2883608 | tf_op jit(solution)/shard_map/stack | solution.py:67
  45.8 1.2 fusion.80
  47.0 1.3 %fusion.81 = (f32[1,2,16,4,1023]{4,3,2,1,0:T(4,128)}, f32[1,2,16,4,1023]{4,3,2,1,0:T(4,128)}) fusion(f32[1,2,16,4,1024]{4,3,2,1,0:T(4,128)S(1)} %maximum_multiply_fusion), kind=kLoop, calls=%fused_computation.131 | loop fusion | bytes 2095104 | tf_op jit(solution)/shard_map/slice | solution.py:37
  48.3 1.3 %collective-permute-start = (f32[1,2,16,1,1024]{4,3,2,1,0:T(1,128)}, f32[1,2,16,1,1024]{4,3,2,1,0:T(1,128)S(1)}, u32[]{:S(2)}, u32[]{:S(2)}) collective-permute-start(f32[1,2,16,1,1024]{4,3,2,1,0:T(1,128)} %get-tuple-element.37), channel_id=1, source_target_pairs={{1,0},{2,1},{3,2},{5,4},{6,5},{7,6},{9,8},{10,9},{11,10},{13,12},{... | collective-permute-start | bytes 393224 | tf_op jit(solution)/shard_map/ppermute | solution.py:24
  49.6 3.7 %collective-permute-start.1 = (f32[1,2,16,1,1024]{4,3,2,1,0:T(1,128)}, f32[1,2,16,1,1024]{4,3,2,1,0:T(1,128)}, u32[]{:S(2)}, u32[]{:S(2)}) collective-permute-start(f32[1,2,16,1,1024]{4,3,2,1,0:T(1,128)} %get-tuple-element.38), channel_id=1, source_target_pairs={{0,1},{1,2},{2,3},{4,5},{5,6},{6,7},{8,9},{9,10},{10,11},{12,13},{... | collective-permute-start | bytes 393224 | tf_op jit(solution)/shard_map/ppermute | solution.py:23
  53.3 1.9 %stack.76 = f32[1,1,16,4,1024]{4,3,2,1,0:T(4,128)} reshape(f32[4,16384]{1,0:T(4,128)} %copy-done.1) | data formatting | bytes 524288 | tf_op jit(solution)/shard_map/stack | solution.py:100
  56.3 2.8 %fusion.24 = f32[1,2,16,4,1024]{4,3,2,1,0:T(4,128)S(1)} fusion(f32[1,2,16,4,1024]{4,3,2,1,0:T(4,128)S(1)} %constant_dynamic-update-slice_fusion, f32[1,2,16,4,1024]{4,3,2,1,0:T(4,128)S(1)} %maximum_multiply_fusion, f32[1,2,16,1,1024]{4,3,2,1,0:T(1,128)} %collective-permute-done.1, f32[1,2,16,1,1024]{4,3,2,1,0:T(1,128)S(1)} %collective-permute-done, ...), kind=kLoop, calls=%fused_computation.32 | loop fusion | flops 2097152 | bytes 5962752 | tf_op jit(solution)/shard_map/sub | solution.py:111
  60.5 1.3 %collective-permute-start.2 = (f32[1,2,16,1,1024]{4,3,2,1,0:T(1,128)S(1)}, f32[1,2,16,1,1024]{4,3,2,1,0:T(1,128)S(1)}, u32[]{:S(2)}, u32[]{:S(2)}) collective-permute-start(f32[1,2,16,1,1024]{4,3,2,1,0:T(1,128)S(1)} %get-tuple-element.31), channel_id=1, source_target_pairs={{1,0},{2,1},{3,2},{5,4},{6,5},{7,6},{9,8},{10,9},{11,10},{13,12},{... | collective-permute-start | bytes 393224 | tf_op jit(solution)/shard_map/ppermute | solution.py:24
  61.8 3.2 %collective-permute-start.3 = (f32[1,2,16,1,1024]{4,3,2,1,0:T(1,128)S(1)}, f32[1,2,16,1,1024]{4,3,2,1,0:T(1,128)S(1)}, u32[]{:S(2)}, u32[]{:S(2)}) collective-permute-start(f32[1,2,16,1,1024]{4,3,2,1,0:T(1,128)S(1)} %get-tuple-element.32), channel_id=1, source_target_pairs={{0,1},{1,2},{2,3},{4,5},{5,6},{6,7},{8,9},{9,10},{10,11},{12,13},{... | collective-permute-start | bytes 393224 | tf_op jit(solution)/shard_map/ppermute | solution.py:23
  65.8 1.2 %fusion.16 = f32[1,2,16,4,1024]{4,3,2,1,0:T(4,128)S(1)} fusion(f32[1,2,16,4,1024]{4,3,2,1,0:T(4,128)S(1)} %constant_dynamic-update-slice_fusion, f32[1,2,16,4,1024]{4,3,2,1,0:T(4,128)S(1)} %fusion.27, f32[1,2,16,1,1024]{4,3,2,1,0:T(1,128)S(1)} %collective-permute-done.3, f32[1,2,16,1,1024]{4,3,2,1,0:T(1,128)S(1)} %collective-permute-done.2, ...), kind=kLoop, calls=%fused_computation.22 | loop fusion | flops 2097152 | bytes 5962752 | tf_op jit(solution)/shard_map/sub | solution.py:111
  68.6 1.3 %collective-permute-start.4 = (f32[1,2,16,1,1024]{4,3,2,1,0:T(1,128)S(1)}, f32[1,2,16,1,1024]{4,3,2,1,0:T(1,128)S(1)}, u32[]{:S(2)}, u32[]{:S(2)}) collective-permute-start(f32[1,2,16,1,1024]{4,3,2,1,0:T(1,128)S(1)} %get-tuple-element.25), channel_id=1, source_target_pairs={{1,0},{2,1},{3,2},{5,4},{6,5},{7,6},{9,8},{10,9},{11,10},{13,12},{... | collective-permute-start | bytes 393224 | tf_op jit(solution)/shard_map/ppermute | solution.py:24
  69.9 5.2 %collective-permute-start.5 = (f32[1,2,16,1,1024]{4,3,2,1,0:T(1,128)S(1)}, f32[1,2,16,1,1024]{4,3,2,1,0:T(1,128)S(1)}, u32[]{:S(2)}, u32[]{:S(2)}) collective-permute-start(f32[1,2,16,1,1024]{4,3,2,1,0:T(1,128)S(1)} %get-tuple-element.26), channel_id=1, source_target_pairs={{0,1},{1,2},{2,3},{4,5},{5,6},{6,7},{8,9},{9,10},{10,11},{12,13},{... | collective-permute-start | bytes 393224 | tf_op jit(solution)/shard_map/ppermute | solution.py:23
  76.1 1.2 %fusion.8 = f32[1,2,16,4,1024]{4,3,2,1,0:T(4,128)S(1)} fusion(f32[1,2,16,4,1024]{4,3,2,1,0:T(4,128)S(1)} %constant_dynamic-update-slice_fusion, f32[1,2,16,4,1024]{4,3,2,1,0:T(4,128)S(1)} %fusion.28, f32[1,2,16,1,1024]{4,3,2,1,0:T(1,128)S(1)} %collective-permute-done.5, f32[1,2,16,1,1024]{4,3,2,1,0:T(1,128)S(1)} %collective-permute-done.4, ...), kind=kLoop, calls=%fused_computation.12 | loop fusion | flops 2097152 | bytes 5962752 | tf_op jit(solution)/shard_map/sub | solution.py:111
  79.3 3.4 %all-to-all-start.3 = ((f32[1,4,16384]{2,0,1:T(1,128)}), f32[1,4,16384]{2,0,1:T(1,128)S(1)}, u32[]{:S(2)}, u32[]{:S(2)}) async-start(f32[1,4,16384]{2,0,1:T(1,128)} %all_to_all.70), calls=%async_computation.3 | async-start | bytes 524288 | tf_op jit(solution)/shard_map/all_to_all | solution.py:115
  83.8 5.8 %all-to-all-done.3 = f32[1,4,16384]{2,0,1:T(1,128)S(1)} async-done(((f32[1,4,16384]{2,0,1:T(1,128)}), f32[1,4,16384]{2,0,1:T(1,128)S(1)}, u32[]{:S(2)}, u32[]{:S(2)}) %all-to-all-start.3) | async-done | bytes 262176 | tf_op jit(solution)/shard_map/all_to_all | solution.py:115
  89.5 5.2 %all-to-all-start.4 = ((f32[1,4,16384]{2,0,1:T(1,128)}), f32[1,4,16384]{2,0,1:T(1,128)S(1)}, u32[]{:S(2)}, u32[]{:S(2)}) async-start(f32[1,4,16384]{2,0,1:T(1,128)} %all_to_all.73), calls=%async_computation.4 | async-start | bytes 524288 | tf_op jit(solution)/shard_map/all_to_all | solution.py:116
  95.4 8.0 %all-to-all-done.4 = f32[1,4,16384]{2,0,1:T(1,128)S(1)} async-done(((f32[1,4,16384]{2,0,1:T(1,128)}), f32[1,4,16384]{2,0,1:T(1,128)S(1)}, u32[]{:S(2)}, u32[]{:S(2)}) %all-to-all-start.4) | async-done | bytes 262176 | tf_op jit(solution)/shard_map/all_to_all | solution.py:116
  105.1 4.0 %all-to-all-start.5 = ((f32[4,1,16384]{2,1,0:T(1,128)}), f32[4,1,16384]{2,1,0:T(1,128)S(1)}, u32[]{:S(2)}, u32[]{:S(2)}) async-start(f32[4,1,16384]{2,1,0:T(1,128)} %copy.6), calls=%async_computation.5 | async-start | bytes 524288 | tf_op jit(solution)/shard_map/all_to_all | solution.py:119
  109.2 10.0 %all-to-all-done.5 = f32[4,1,16384]{2,1,0:T(1,128)S(1)} async-done(((f32[4,1,16384]{2,1,0:T(1,128)}), f32[4,1,16384]{2,1,0:T(1,128)S(1)}, u32[]{:S(2)}, u32[]{:S(2)}) %all-to-all-start.5) | async-done | bytes 262176 | tf_op jit(solution)/shard_map/all_to_all | solution.py:119
  (56 shorter events, 24.4 us)
Async XLA Ops:
  18.1 11.4 %all-to-all-start.1 = ((f32[4,1,16384]{2,1,0:T(1,128)}), f32[4,1,16384]{2,1,0:T(1,128)S(1)}, u32[]{:S(2)}, u32[]{:S(2)}) async-start(f32[4,1,16384]{2,1,0:T(1,128)} %copy.4), calls=%async_computation.1 | async-start | bytes 524288 | tf_op jit(solution)/shard_map/all_to_all | solution.py:97
  29.5 10.2 %all-to-all-start.2 = ((f32[4,1,16384]{2,1,0:T(1,128)}), f32[4,1,16384]{2,1,0:T(1,128)S(1)}, u32[]{:S(2)}, u32[]{:S(2)}) async-start(f32[4,1,16384]{2,1,0:T(1,128)} %copy.5), calls=%async_computation.2 | async-start | bytes 524288 | tf_op jit(solution)/shard_map/all_to_all | solution.py:98
  33.0 0.7 copy-start.4
  40.3 0.7 copy-start.1
  40.3 1.0 copy-start
  47.0 6.3 %copy-start.3 = (f32[1,1,16,4,1024]{4,3,2,1,0:T(4,128)S(1)}, f32[1,1,16,4,1024]{4,3,2,1,0:T(4,128)}, u32[]{:S(2)}) copy-start(f32[1,1,16,4,1024]{4,3,2,1,0:T(4,128)} %stack.75) | copy-start | bytes 786436
  48.3 7.9 %collective-permute-start = (f32[1,2,16,1,1024]{4,3,2,1,0:T(1,128)}, f32[1,2,16,1,1024]{4,3,2,1,0:T(1,128)S(1)}, u32[]{:S(2)}, u32[]{:S(2)}) collective-permute-start(f32[1,2,16,1,1024]{4,3,2,1,0:T(1,128)} %get-tuple-element.37), channel_id=1, source_target_pairs={{1,0},{2,1},{3,2},{5,4},{6,5},{7,6},{9,8},{10,9},{11,10},{13,12},{... | collective-permute-start | bytes 393224 | tf_op jit(solution)/shard_map/ppermute | solution.py:24
  49.6 6.7 %collective-permute-start.1 = (f32[1,2,16,1,1024]{4,3,2,1,0:T(1,128)}, f32[1,2,16,1,1024]{4,3,2,1,0:T(1,128)}, u32[]{:S(2)}, u32[]{:S(2)}) collective-permute-start(f32[1,2,16,1,1024]{4,3,2,1,0:T(1,128)} %get-tuple-element.38), channel_id=1, source_target_pairs={{0,1},{1,2},{2,3},{4,5},{5,6},{6,7},{8,9},{9,10},{10,11},{12,13},{... | collective-permute-start | bytes 393224 | tf_op jit(solution)/shard_map/ppermute | solution.py:23
  55.1 1.1 copy-start.2
  60.5 4.7 %collective-permute-start.2 = (f32[1,2,16,1,1024]{4,3,2,1,0:T(1,128)S(1)}, f32[1,2,16,1,1024]{4,3,2,1,0:T(1,128)S(1)}, u32[]{:S(2)}, u32[]{:S(2)}) collective-permute-start(f32[1,2,16,1,1024]{4,3,2,1,0:T(1,128)S(1)} %get-tuple-element.31), channel_id=1, source_target_pairs={{1,0},{2,1},{3,2},{5,4},{6,5},{7,6},{9,8},{10,9},{11,10},{13,12},{... | collective-permute-start | bytes 393224 | tf_op jit(solution)/shard_map/ppermute | solution.py:24
  61.8 4.0 %collective-permute-start.3 = (f32[1,2,16,1,1024]{4,3,2,1,0:T(1,128)S(1)}, f32[1,2,16,1,1024]{4,3,2,1,0:T(1,128)S(1)}, u32[]{:S(2)}, u32[]{:S(2)}) collective-permute-start(f32[1,2,16,1,1024]{4,3,2,1,0:T(1,128)S(1)} %get-tuple-element.32), channel_id=1, source_target_pairs={{0,1},{1,2},{2,3},{4,5},{5,6},{6,7},{8,9},{9,10},{10,11},{12,13},{... | collective-permute-start | bytes 393224 | tf_op jit(solution)/shard_map/ppermute | solution.py:23
  68.6 6.7 %collective-permute-start.4 = (f32[1,2,16,1,1024]{4,3,2,1,0:T(1,128)S(1)}, f32[1,2,16,1,1024]{4,3,2,1,0:T(1,128)S(1)}, u32[]{:S(2)}, u32[]{:S(2)}) collective-permute-start(f32[1,2,16,1,1024]{4,3,2,1,0:T(1,128)S(1)} %get-tuple-element.25), channel_id=1, source_target_pairs={{1,0},{2,1},{3,2},{5,4},{6,5},{7,6},{9,8},{10,9},{11,10},{13,12},{... | collective-permute-start | bytes 393224 | tf_op jit(solution)/shard_map/ppermute | solution.py:24
  69.9 6.2 %collective-permute-start.5 = (f32[1,2,16,1,1024]{4,3,2,1,0:T(1,128)S(1)}, f32[1,2,16,1,1024]{4,3,2,1,0:T(1,128)S(1)}, u32[]{:S(2)}, u32[]{:S(2)}) collective-permute-start(f32[1,2,16,1,1024]{4,3,2,1,0:T(1,128)S(1)} %get-tuple-element.26), channel_id=1, source_target_pairs={{0,1},{1,2},{2,3},{4,5},{5,6},{6,7},{8,9},{9,10},{10,11},{12,13},{... | collective-permute-start | bytes 393224 | tf_op jit(solution)/shard_map/ppermute | solution.py:23
  79.3 10.3 %all-to-all-start.3 = ((f32[1,4,16384]{2,0,1:T(1,128)}), f32[1,4,16384]{2,0,1:T(1,128)S(1)}, u32[]{:S(2)}, u32[]{:S(2)}) async-start(f32[1,4,16384]{2,0,1:T(1,128)} %all_to_all.70), calls=%async_computation.3 | async-start | bytes 524288 | tf_op jit(solution)/shard_map/all_to_all | solution.py:115
  89.5 13.9 %all-to-all-start.4 = ((f32[1,4,16384]{2,0,1:T(1,128)}), f32[1,4,16384]{2,0,1:T(1,128)S(1)}, u32[]{:S(2)}, u32[]{:S(2)}) async-start(f32[1,4,16384]{2,0,1:T(1,128)} %all_to_all.73), calls=%async_computation.4 | async-start | bytes 524288 | tf_op jit(solution)/shard_map/all_to_all | solution.py:116
  105.1 14.1 %all-to-all-start.5 = ((f32[4,1,16384]{2,1,0:T(1,128)}), f32[4,1,16384]{2,1,0:T(1,128)S(1)}, u32[]{:S(2)}, u32[]{:S(2)}) async-start(f32[4,1,16384]{2,1,0:T(1,128)} %copy.6), calls=%async_computation.5 | async-start | bytes 524288 | tf_op jit(solution)/shard_map/all_to_all | solution.py:119
where the time goes:
time: 122 us; the launch traced here: 121 us
  starting transfers between devices  35.5 us (29%)
  waiting for transfers between devices  34.8 us (29%)
  local copies, waits for them, and re-layouts  17.9 us (15%)
  blocking collectives  15 us (12%)
  other arithmetic  14.3 us (12%)
  matrix products  2.78 us (2%)
    all_to_all x1, blocking collectives, local(): lax.all_to_all(scaled, 'tm', split_axis=1, concat_axis=0, tiled=True)  15 us
    ppermute x3, starting transfers between devices, padded(): before = lax.ppermute(last, axis, up)  12.1 us
    all_to_all x1, waiting for transfers between devices, local(): lax.all_to_all(values, 'tm', split_axis=0, concat_axis=1, tiled=True)  10 us
    all_to_all x1, waiting for transfers between devices, local(): lax.all_to_all(field_im, 'tm', split_axis=1, concat_axis=0, tiled=True)  8 us
    all_to_all x1, waiting for transfers between devices, local(): lax.all_to_all(spectrum_re, 'tm', split_axis=0, concat_axis=1, tiled=True)  6.28 us
    all_to_all x1, waiting for transfers between devices, local(): lax.all_to_all(field_re, 'tm', split_axis=1, concat_axis=0, tiled=True)  5.78 us
    sub x3, other arithmetic, local(): source - applied  5.27 us
    all_to_all x1, starting transfers between devices, local(): lax.all_to_all(field_im, 'tm', split_axis=1, concat_axis=0, tiled=True)  5.19 us
  transfers between devices with their start and end apart: 11, of which 7 were waited for; matrix products, arithmetic and copies ran while one was open for 7% of the time, Pallas kernels for 0%

commit v1 on v0

--- a/solution.py
+++ b/solution.py
@@ -11,6 +11,18 @@
     1.0 / (1.0 - 0.5 * math.cos(5.0 * math.pi / 8.0)),
     1.0 / (1.0 - 0.5 * math.cos(7.0 * math.pi / 8.0)),
 )
+
+
+def move_modes(sample, ndim_at, vec):
+    moved = sample.shape
+    d_next = sample.reshape(*moved[:ndim_at], vec, moved[ndim_at] // vec, *moved[ndim_at + 1 :])
+    return jnp.moveaxis(d_next, ndim_at, 0)
+
+
+def forms_advance(xx, d_out):
+    xx = jnp.moveaxis(xx, 0, d_out)
+    y = xx.shape
+    return xx.reshape(*y[:d_out], y[d_out] * y[d_out + 1], *y[d_out + 2 :])
 
 
 def padded(shard, sides, width):
@@ -78,6 +90,22 @@
 
 
 def local(rhs, diffusivity, velocity):
+
+    def pack_the_slots(sheet, along_axis, s0, buf):
+        arr_now = lax.psum(1, along_axis)
+        mixed_arr = lax.axis_index(along_axis)
+        near, next_value = (arr_now, mixed_arr)
+        item_now = move_modes(sheet, s0, near)
+        src_i = 1
+        store = [item_now[next_value]]
+        while src_i < near:
+            val = item_now[next_value ^ src_i]
+            store.append(lax.ppermute(val, along_axis, [(p, p ^ src_i) for p in range(near)]))
+            src_i += 1
+        f_now = jnp.stack(store, 0)
+        item_now = f_now[next_value ^ jnp.arange(near)]
+        return forms_advance(item_now, buf)
+
     local_steps, depth, rows_y, rows_x = rhs.shape
     length = local_steps * lax.axis_size("tm")
     first_step = lax.axis_index("tm") * local_steps
@@ -95,7 +123,7 @@
     spectrum_im = -highest(sine_table, regrouped)
     source_re, source_im = (
         lax.all_to_all(spectrum_re, "tm", split_axis=0, concat_axis=1, tiled=True),
-        lax.all_to_all(spectrum_im, "tm", split_axis=0, concat_axis=1, tiled=True),
+        pack_the_slots(spectrum_im, "tm", 0, 1),
     )
     source = jnp.stack([source_re, source_im], axis=1).reshape(
         local_steps, 2, depth, rows_y, rows_x

time: 122 us -> 112 us (0.918)
  blocking collectives: 15 us -> 0 us
  starting transfers between devices: 35.5 us -> 44.5 us
  local copies, waits for them, and re-layouts: 17.9 us -> 12.4 us
  waiting for transfers between devices: 34.8 us -> 38.8 us
  other arithmetic: 14.3 us -> 11.6 us
    all_to_all x1 -> x0, blocking collectives: 15 us -> none  [local(): lax.all_to_all(scaled, 'tm', split_axis=1, concat_axis=0, tiled=True)]
    ppermute x0 -> x3, starting transfers between devices: none -> 4.45 us  [pack_the_slots(): lax.ppermute(val, along_axis, [(p, p ^ src_i) for p in range(near)])]
    all_to_all x1, waiting for transfers between devices: 3.39 us -> 7.38 us  [local(): lax.all_to_all(scaled, 'tm', split_axis=1, concat_axis=0, tiled=True)]
    another operation x3, local copies, waits for them, and re-layouts: 3.85 us -> 0.49 us  [local(): jnp.stack([source_re, source_im], axis=1)]
    all_to_all x1, starting transfers between devices: 3.4 us -> 6.35 us  [local(): lax.all_to_all(scaled, 'tm', split_axis=1, concat_axis=0, tiled=True)]
    ppermute x3, starting transfers between devices: 12.1 us -> 13.8 us  [padded(): before = lax.ppermute(last, axis, up)]
    sub x3, other arithmetic: 5.27 us -> 3.68 us  [local(): source - applied]
  transfers between devices with their start and end apart: 11 -> 14, of which waited for: 7 -> 8; matrix products, arithmetic and copies ran while one was open for 7% -> 4% of each run, Pallas kernels for 0% -> 0%
where the time goes in v1:
time: 112 us; the launch traced here: 111 us
  starting transfers between devices  44.5 us (40%)
  waiting for transfers between devices  38.8 us (35%)
  local copies, waits for them, and re-layouts  12.4 us (11%)
  other arithmetic  11.6 us (10%)
  matrix products  2.78 us (2%)
    ppermute x3, starting transfers between devices, padded(): before = lax.ppermute(last, axis, up)  13.8 us
    all_to_all x1, waiting for transfers between devices, local(): lax.all_to_all(values, 'tm', split_axis=0, concat_axis=1, tiled=True)  10 us
    all_to_all x1, waiting for transfers between devices, local(): lax.all_to_all(field_im, 'tm', split_axis=1, concat_axis=0, tiled=True)  8 us
    all_to_all x1, waiting for transfers between devices, local(): lax.all_to_all(scaled, 'tm', split_axis=1, concat_axis=0, tiled=True)  7.38 us
    all_to_all x1, starting transfers between devices, local(): lax.all_to_all(scaled, 'tm', split_axis=1, concat_axis=0, tiled=True)  6.35 us
    all_to_all x1, waiting for transfers between devices, local(): lax.all_to_all(field_re, 'tm', split_axis=1, concat_axis=0, tiled=True)  5.8 us
    all_to_all x1, waiting for transfers between devices, local(): lax.all_to_all(spectrum_re, 'tm', split_axis=0, concat_axis=1, tiled=True)  5.31 us
    all_to_all x1, starting transfers between devices, local(): lax.all_to_all(field_im, 'tm', split_axis=1, concat_axis=0, tiled=True)  5.19 us
  transfers between devices with their start and end apart: 14, of which 8 were waited for; matrix products, arithmetic and copies ran while one was open for 4% of the time, Pallas kernels for 0%

profile of v1, /device:TPU:0, one launch (start us, length us, event | category | flops | bytes accessed | tf_op | source)
XLA Modules:
  0.0 110.8 jit_solution(17991014469948569229)
XLA Ops:
  1.0 1.1 mul.497
  2.1 6.3 %all-to-all-start = ((f32[1,4,16384]{2,0,1:T(1,128)}), f32[1,4,16384]{2,0,1:T(1,128)S(1)}, u32[]{:S(2)}, u32[]{:S(2)}) async-start(f32[1,4,16384]{2,0,1:T(1,128)} %mul.497), calls=%async_computation | async-start | bytes 524288 | tf_op jit(solution)/shard_map/all_to_all | solution.py:119
  10.0 7.4 %all-to-all-done = f32[1,4,16384]{2,0,1:T(1,128)S(1)} async-done(((f32[1,4,16384]{2,0,1:T(1,128)}), f32[1,4,16384]{2,0,1:T(1,128)S(1)}, u32[]{:S(2)}, u32[]{:S(2)}) %all-to-all-start) | async-done | bytes 262176 | tf_op jit(solution)/shard_map/all_to_all | solution.py:119
  18.3 1.5 %collective-permute-start.2 = (f32[1,16384]{1,0:T(1,128)S(1)}, f32[1,16384]{1,0:T(1,128)S(1)}, u32[]{:S(2)}, u32[]{:S(2)}) collective-permute-start(f32[1,16384]{1,0:T(1,128)S(1)} %get-tuple-element.46), channel_id=1, source_target_pairs={{0,12},{4,8},{8,4},{12,0},{1,13},{5,9},{9,5},{13,1},{2,14},{6,10},... | collective-permute-start | bytes 196616 | tf_op jit(solution)/shard_map/ppermute | solution.py:103
  20.0 2.8 %collective-permute-start = (f32[1,16384]{1,0:T(1,128)S(1)}, f32[1,16384]{1,0:T(1,128)S(1)}, u32[]{:S(2)}, u32[]{:S(2)}) collective-permute-start(f32[1,16384]{1,0:T(1,128)S(1)} %get-tuple-element.48), channel_id=1, source_target_pairs={{0,4},{4,0},{8,12},{12,8},{1,5},{5,1},{9,13},{13,9},{2,6},{6,2},{1... | collective-permute-start | bytes 196616 | tf_op jit(solution)/shard_map/ppermute | solution.py:103
  24.4 3.4 %all-to-all-start.1 = ((f32[4,1,16384]{2,1,0:T(1,128)}), f32[4,1,16384]{2,1,0:T(1,128)S(1)}, u32[]{:S(2)}, u32[]{:S(2)}) async-start(f32[4,1,16384]{2,1,0:T(1,128)} %copy.4), calls=%async_computation.1 | async-start | bytes 524288 | tf_op jit(solution)/shard_map/all_to_all | solution.py:125
  29.3 5.3 %all-to-all-done.1 = f32[4,1,16384]{2,1,0:T(1,128)S(1)} async-done(((f32[4,1,16384]{2,1,0:T(1,128)}), f32[4,1,16384]{2,1,0:T(1,128)S(1)}, u32[]{:S(2)}, u32[]{:S(2)}) %all-to-all-start.1) | async-done | bytes 262176 | tf_op jit(solution)/shard_map/all_to_all | solution.py:125
  36.5 2.4 %fusion.37 = (f32[1,1,16,4,1024]{4,3,2,1,0:T(4,128)S(1)}, f32[1,1,16,4,1024]{4,3,2,1,0:T(4,128)S(1)}, f32[16,4,1024]{2,1,0:T(4,128)S(1)}, f32[16,4,1024]{2,1,0:T...) fusion(f32[16,4,1024]{2,1,0:T(4,128)S(1)} %squeeze.79, ...), kind=kLoop, calls=%fused_computation.80 | loop fusion | flops 1179648 | bytes 2883608 | tf_op jit(solution)/shard_map/stack | solution.py:79
  40.1 1.3 %collective-permute-start.3 = (f32[1,2,16,1,1024]{4,3,2,1,0:T(1,128)S(1)}, f32[1,2,16,1,1024]{4,3,2,1,0:T(1,128)S(1)}, u32[]{:S(2)}, u32[]{:S(2)}) collective-permute-start(f32[1,2,16,1,1024]{4,3,2,1,0:T(1,128)S(1)} %get-tuple-element.37), channel_id=1, source_target_pairs={{1,0},{2,1},{3,2},{5,4},{6,5},{7,6},{9,8},{10,9},{11,10},{13,12},{... | collective-permute-start | bytes 393224 | tf_op jit(solution)/shard_map/ppermute | solution.py:36
  41.4 3.0 %collective-permute-start.4 = (f32[1,2,16,1,1024]{4,3,2,1,0:T(1,128)S(1)}, f32[1,2,16,1,1024]{4,3,2,1,0:T(1,128)S(1)}, u32[]{:S(2)}, u32[]{:S(2)}) collective-permute-start(f32[1,2,16,1,1024]{4,3,2,1,0:T(1,128)S(1)} %get-tuple-element.38), channel_id=1, source_target_pairs={{0,1},{1,2},{2,3},{4,5},{5,6},{6,7},{8,9},{9,10},{10,11},{12,13},{... | collective-permute-start | bytes 393224 | tf_op jit(solution)/shard_map/ppermute | solution.py:35
  45.4 1.2 %fusion.23 = f32[1,2,16,4,1024]{4,3,2,1,0:T(4,128)S(1)} fusion(f32[1,2,16,4,1024]{4,3,2,1,0:T(4,128)S(1)} %constant_dynamic-update-slice_fusion, f32[1,2,16,4,1024]{4,3,2,1,0:T(4,128)S(1)} %maximum_multiply_fusion, f32[1,2,16,1,1024]{4,3,2,1,0:T(1,128)S(1)} %collective-permute-done.4, f32[1,2,16,1,1024]{4,3,2,1,0:T(1,128)S(1)} %collective-permute-done.3, ...), kind=kLoop, calls=%fused_computation.32 | loop fusion | flops 2097152 | bytes 5962752 | tf_op jit(solution)/shard_map/sub | solution.py:139
  48.1 1.3 %collective-permute-start.5 = (f32[1,2,16,1,1024]{4,3,2,1,0:T(1,128)S(1)}, f32[1,2,16,1,1024]{4,3,2,1,0:T(1,128)S(1)}, u32[]{:S(2)}, u32[]{:S(2)}) collective-permute-start(f32[1,2,16,1,1024]{4,3,2,1,0:T(1,128)S(1)} %get-tuple-element.31), channel_id=1, source_target_pairs={{1,0},{2,1},{3,2},{5,4},{6,5},{7,6},{9,8},{10,9},{11,10},{13,12},{... | collective-permute-start | bytes 393224 | tf_op jit(solution)/shard_map/ppermute | solution.py:36
  49.4 4.8 %collective-permute-start.6 = (f32[1,2,16,1,1024]{4,3,2,1,0:T(1,128)S(1)}, f32[1,2,16,1,1024]{4,3,2,1,0:T(1,128)S(1)}, u32[]{:S(2)}, u32[]{:S(2)}) collective-permute-start(f32[1,2,16,1,1024]{4,3,2,1,0:T(1,128)S(1)} %get-tuple-element.32), channel_id=1, source_target_pairs={{0,1},{1,2},{2,3},{4,5},{5,6},{6,7},{8,9},{9,10},{10,11},{12,13},{... | collective-permute-start | bytes 393224 | tf_op jit(solution)/shard_map/ppermute | solution.py:35
  55.0 1.2 %fusion.15 = f32[1,2,16,4,1024]{4,3,2,1,0:T(4,128)S(1)} fusion(f32[1,2,16,4,1024]{4,3,2,1,0:T(4,128)S(1)} %constant_dynamic-update-slice_fusion, f32[1,2,16,4,1024]{4,3,2,1,0:T(4,128)S(1)} %fusion.26, f32[1,2,16,1,1024]{4,3,2,1,0:T(1,128)S(1)} %collective-permute-done.6, f32[1,2,16,1,1024]{4,3,2,1,0:T(1,128)S(1)} %collective-permute-done.5, ...), kind=kLoop, calls=%fused_computation.22 | loop fusion | flops 2097152 | bytes 5962752 | tf_op jit(solution)/shard_map/sub | solution.py:139
  57.7 1.3 %collective-permute-start.7 = (f32[1,2,16,1,1024]{4,3,2,1,0:T(1,128)S(1)}, f32[1,2,16,1,1024]{4,3,2,1,0:T(1,128)S(1)}, u32[]{:S(2)}, u32[]{:S(2)}) collective-permute-start(f32[1,2,16,1,1024]{4,3,2,1,0:T(1,128)S(1)} %get-tuple-element.25), channel_id=1, source_target_pairs={{1,0},{2,1},{3,2},{5,4},{6,5},{7,6},{9,8},{10,9},{11,10},{13,12},{... | collective-permute-start | bytes 393224 | tf_op jit(solution)/shard_map/ppermute | solution.py:36
  59.0 5.9 %collective-permute-start.8 = (f32[1,2,16,1,1024]{4,3,2,1,0:T(1,128)S(1)}, f32[1,2,16,1,1024]{4,3,2,1,0:T(1,128)S(1)}, u32[]{:S(2)}, u32[]{:S(2)}) collective-permute-start(f32[1,2,16,1,1024]{4,3,2,1,0:T(1,128)S(1)} %get-tuple-element.26), channel_id=1, source_target_pairs={{0,1},{1,2},{2,3},{4,5},{5,6},{6,7},{8,9},{9,10},{10,11},{12,13},{... | collective-permute-start | bytes 393224 | tf_op jit(solution)/shard_map/ppermute | solution.py:35
  66.0 1.2 %fusion.7 = f32[1,2,16,4,1024]{4,3,2,1,0:T(4,128)S(1)} fusion(f32[1,2,16,4,1024]{4,3,2,1,0:T(4,128)S(1)} %constant_dynamic-update-slice_fusion, f32[1,2,16,4,1024]{4,3,2,1,0:T(4,128)S(1)} %fusion.27, f32[1,2,16,1,1024]{4,3,2,1,0:T(1,128)S(1)} %collective-permute-done.8, f32[1,2,16,1,1024]{4,3,2,1,0:T(1,128)S(1)} %collective-permute-done.7, ...), kind=kLoop, calls=%fused_computation.12 | loop fusion | flops 2097152 | bytes 5962752 | tf_op jit(solution)/shard_map/sub | solution.py:139
  68.1 1.1 all_to_all.58
  69.1 3.4 %all-to-all-start.2 = ((f32[1,4,16384]{2,0,1:T(1,128)}), f32[1,4,16384]{2,0,1:T(1,128)S(1)}, u32[]{:S(2)}, u32[]{:S(2)}) async-start(f32[1,4,16384]{2,0,1:T(1,128)} %all_to_all.58), calls=%async_computation.2 | async-start | bytes 524288 | tf_op jit(solution)/shard_map/all_to_all | solution.py:143
  73.6 5.8 %all-to-all-done.2 = f32[1,4,16384]{2,0,1:T(1,128)S(1)} async-done(((f32[1,4,16384]{2,0,1:T(1,128)}), f32[1,4,16384]{2,0,1:T(1,128)S(1)}, u32[]{:S(2)}, u32[]{:S(2)}) %all-to-all-start.2) | async-done | bytes 262176 | tf_op jit(solution)/shard_map/all_to_all | solution.py:143
  79.4 5.2 %all-to-all-start.3 = ((f32[1,4,16384]{2,0,1:T(1,128)}), f32[1,4,16384]{2,0,1:T(1,128)S(1)}, u32[]{:S(2)}, u32[]{:S(2)}) async-start(f32[1,4,16384]{2,0,1:T(1,128)} %all_to_all.61), calls=%async_computation.3 | async-start | bytes 524288 | tf_op jit(solution)/shard_map/all_to_all | solution.py:144
  85.3 8.0 %all-to-all-done.3 = f32[1,4,16384]{2,0,1:T(1,128)S(1)} async-done(((f32[1,4,16384]{2,0,1:T(1,128)}), f32[1,4,16384]{2,0,1:T(1,128)S(1)}, u32[]{:S(2)}, u32[]{:S(2)}) %all-to-all-start.3) | async-done | bytes 262176 | tf_op jit(solution)/shard_map/all_to_all | solution.py:144
  95.0 4.0 %all-to-all-start.4 = ((f32[4,1,16384]{2,1,0:T(1,128)}), f32[4,1,16384]{2,1,0:T(1,128)S(1)}, u32[]{:S(2)}, u32[]{:S(2)}) async-start(f32[4,1,16384]{2,1,0:T(1,128)} %copy.5), calls=%async_computation.4 | async-start | bytes 524288 | tf_op jit(solution)/shard_map/all_to_all | solution.py:147
  99.1 10.0 %all-to-all-done.4 = f32[4,1,16384]{2,1,0:T(1,128)S(1)} async-done(((f32[4,1,16384]{2,1,0:T(1,128)}), f32[4,1,16384]{2,1,0:T(1,128)S(1)}, u32[]{:S(2)}, u32[]{:S(2)}) %all-to-all-start.4) | async-done | bytes 262176 | tf_op jit(solution)/shard_map/all_to_all | solution.py:147
  (58 shorter events, 21.0 us)
Async XLA Ops:
  2.1 15.3 %all-to-all-start = ((f32[1,4,16384]{2,0,1:T(1,128)}), f32[1,4,16384]{2,0,1:T(1,128)S(1)}, u32[]{:S(2)}, u32[]{:S(2)}) async-start(f32[1,4,16384]{2,0,1:T(1,128)} %mul.497), calls=%async_computation | async-start | bytes 524288 | tf_op jit(solution)/shard_map/all_to_all | solution.py:119
  8.6 0.7 copy-start.1
  18.3 9.5 %collective-permute-start.2 = (f32[1,16384]{1,0:T(1,128)S(1)}, f32[1,16384]{1,0:T(1,128)S(1)}, u32[]{:S(2)}, u32[]{:S(2)}) collective-permute-start(f32[1,16384]{1,0:T(1,128)S(1)} %get-tuple-element.46), channel_id=1, source_target_pairs={{0,12},{4,8},{8,4},{12,0},{1,13},{5,9},{9,5},{13,1},{2,14},{6,10},... | collective-permute-start | bytes 196616 | tf_op jit(solution)/shard_map/ppermute | solution.py:103
  19.8 8.1 %collective-permute-start.1 = (f32[1,16384]{1,0:T(1,128)S(1)}, f32[1,16384]{1,0:T(1,128)S(1)}, u32[]{:S(2)}, u32[]{:S(2)}) collective-permute-start(f32[1,16384]{1,0:T(1,128)S(1)} %get-tuple-element.47), channel_id=1, source_target_pairs={{0,8},{4,12},{8,0},{12,4},{1,9},{5,13},{9,1},{13,5},{2,10},{6,14},... | collective-permute-start | bytes 196616 | tf_op jit(solution)/shard_map/ppermute | solution.py:103
  20.0 7.9 %collective-permute-start = (f32[1,16384]{1,0:T(1,128)S(1)}, f32[1,16384]{1,0:T(1,128)S(1)}, u32[]{:S(2)}, u32[]{:S(2)}) collective-permute-start(f32[1,16384]{1,0:T(1,128)S(1)} %get-tuple-element.48), channel_id=1, source_target_pairs={{0,4},{4,0},{8,12},{12,8},{1,5},{5,1},{9,13},{13,9},{2,6},{6,2},{1... | collective-permute-start | bytes 196616 | tf_op jit(solution)/shard_map/ppermute | solution.py:103
  24.4 10.2 %all-to-all-start.1 = ((f32[4,1,16384]{2,1,0:T(1,128)}), f32[4,1,16384]{2,1,0:T(1,128)S(1)}, u32[]{:S(2)}, u32[]{:S(2)}) async-start(f32[4,1,16384]{2,1,0:T(1,128)} %copy.4), calls=%async_computation.1 | async-start | bytes 524288 | tf_op jit(solution)/shard_map/all_to_all | solution.py:125
  35.5 1.0 copy-start
  40.1 4.4 %collective-permute-start.3 = (f32[1,2,16,1,1024]{4,3,2,1,0:T(1,128)S(1)}, f32[1,2,16,1,1024]{4,3,2,1,0:T(1,128)S(1)}, u32[]{:S(2)}, u32[]{:S(2)}) collective-permute-start(f32[1,2,16,1,1024]{4,3,2,1,0:T(1,128)S(1)} %get-tuple-element.37), channel_id=1, source_target_pairs={{1,0},{2,1},{3,2},{5,4},{6,5},{7,6},{9,8},{10,9},{11,10},{13,12},{... | collective-permute-start | bytes 393224 | tf_op jit(solution)/shard_map/ppermute | solution.py:36
  41.4 4.0 %collective-permute-start.4 = (f32[1,2,16,1,1024]{4,3,2,1,0:T(1,128)S(1)}, f32[1,2,16,1,1024]{4,3,2,1,0:T(1,128)S(1)}, u32[]{:S(2)}, u32[]{:S(2)}) collective-permute-start(f32[1,2,16,1,1024]{4,3,2,1,0:T(1,128)S(1)} %get-tuple-element.38), channel_id=1, source_target_pairs={{0,1},{1,2},{2,3},{4,5},{5,6},{6,7},{8,9},{9,10},{10,11},{12,13},{... | collective-permute-start | bytes 393224 | tf_op jit(solution)/shard_map/ppermute | solution.py:35
  48.1 6.3 %collective-permute-start.5 = (f32[1,2,16,1,1024]{4,3,2,1,0:T(1,128)S(1)}, f32[1,2,16,1,1024]{4,3,2,1,0:T(1,128)S(1)}, u32[]{:S(2)}, u32[]{:S(2)}) collective-permute-start(f32[1,2,16,1,1024]{4,3,2,1,0:T(1,128)S(1)} %get-tuple-element.31), channel_id=1, source_target_pairs={{1,0},{2,1},{3,2},{5,4},{6,5},{7,6},{9,8},{10,9},{11,10},{13,12},{... | collective-permute-start | bytes 393224 | tf_op jit(solution)/shard_map/ppermute | solution.py:36
  49.4 5.6 %collective-permute-start.6 = (f32[1,2,16,1,1024]{4,3,2,1,0:T(1,128)S(1)}, f32[1,2,16,1,1024]{4,3,2,1,0:T(1,128)S(1)}, u32[]{:S(2)}, u32[]{:S(2)}) collective-permute-start(f32[1,2,16,1,1024]{4,3,2,1,0:T(1,128)S(1)} %get-tuple-element.32), channel_id=1, source_target_pairs={{0,1},{1,2},{2,3},{4,5},{5,6},{6,7},{8,9},{9,10},{10,11},{12,13},{... | collective-permute-start | bytes 393224 | tf_op jit(solution)/shard_map/ppermute | solution.py:35
  57.7 7.4 %collective-permute-start.7 = (f32[1,2,16,1,1024]{4,3,2,1,0:T(1,128)S(1)}, f32[1,2,16,1,1024]{4,3,2,1,0:T(1,128)S(1)}, u32[]{:S(2)}, u32[]{:S(2)}) collective-permute-start(f32[1,2,16,1,1024]{4,3,2,1,0:T(1,128)S(1)} %get-tuple-element.25), channel_id=1, source_target_pairs={{1,0},{2,1},{3,2},{5,4},{6,5},{7,6},{9,8},{10,9},{11,10},{13,12},{... | collective-permute-start | bytes 393224 | tf_op jit(solution)/shard_map/ppermute | solution.py:36
  59.0 6.9 %collective-permute-start.8 = (f32[1,2,16,1,1024]{4,3,2,1,0:T(1,128)S(1)}, f32[1,2,16,1,1024]{4,3,2,1,0:T(1,128)S(1)}, u32[]{:S(2)}, u32[]{:S(2)}) collective-permute-start(f32[1,2,16,1,1024]{4,3,2,1,0:T(1,128)S(1)} %get-tuple-element.26), channel_id=1, source_target_pairs={{0,1},{1,2},{2,3},{4,5},{5,6},{6,7},{8,9},{9,10},{10,11},{12,13},{... | collective-permute-start | bytes 393224 | tf_op jit(solution)/shard_map/ppermute | solution.py:35
  69.1 10.3 %all-to-all-start.2 = ((f32[1,4,16384]{2,0,1:T(1,128)}), f32[1,4,16384]{2,0,1:T(1,128)S(1)}, u32[]{:S(2)}, u32[]{:S(2)}) async-start(f32[1,4,16384]{2,0,1:T(1,128)} %all_to_all.58), calls=%async_computation.2 | async-start | bytes 524288 | tf_op jit(solution)/shard_map/all_to_all | solution.py:143
  79.4 13.9 %all-to-all-start.3 = ((f32[1,4,16384]{2,0,1:T(1,128)}), f32[1,4,16384]{2,0,1:T(1,128)S(1)}, u32[]{:S(2)}, u32[]{:S(2)}) async-start(f32[1,4,16384]{2,0,1:T(1,128)} %all_to_all.61), calls=%async_computation.3 | async-start | bytes 524288 | tf_op jit(solution)/shard_map/all_to_all | solution.py:144
  95.0 14.1 %all-to-all-start.4 = ((f32[4,1,16384]{2,1,0:T(1,128)}), f32[4,1,16384]{2,1,0:T(1,128)S(1)}, u32[]{:S(2)}, u32[]{:S(2)}) async-start(f32[4,1,16384]{2,1,0:T(1,128)} %copy.5), calls=%async_computation.4 | async-start | bytes 524288 | tf_op jit(solution)/shard_map/all_to_all | solution.py:147
